TPU v7x, 512 devices: a whole 4x4x16 slice. The times are simulated.
512 devices in a mesh: blk: 128 (over y_hi, z, x), feat: 4 (over y_lo, core).
Axes of the slice: x: 4, y: 4 (y_hi: 2, y_lo: 2; y = y_hi * 2 + y_lo), z: 16, core: 2. Of those that a mesh axis runs over, the one named last changes fastest.
Arguments:
- features: bfloat16 [256, 131072], P('feat', 'blk'), may hold values from -6 to 6
- block_values: bfloat16 [17408, 128, 128], P('blk'), may hold values from 0 to 1, as said below
- block_rows: int32 [17408], P('blk'), may hold values from 0 to 7, as said below
- block_cols: int32 [17408], P('blk'), may hold values from 0 to 1023, as said below
- block_count: int32 [128], P('blk'), may hold values from 8 to 136, as said below
- labels: int32 [131072], P(('blk', 'feat')), may hold values from 0 to 127
- weight_in: bfloat16 [256, 256], replicated, may hold values from -0.375 to 0.375
- weight_out: bfloat16 [256, 128], replicated, may hold values from -1 to 1
Outputs:
- logits: float32 [128, 131072], P(None, ('blk', 'feat'))
- grad_in: float32 [256, 256], replicated
- grad_out: float32 [256, 128], replicated
Inputs may be any that keep to these rules, and one draw needn't show every extreme that they name: The first block_count[s] slots of stripe s are its blocks; the remaining slots hold blocks that are not part of the matrix; every stripe holds its 8 diagonal blocks, and the busiest stripe fills all 136 slots. `block_rows`: block row of a slot inside its stripe. `block_cols`: every slot's block column lies within 8 blocks of its global block row, counted around the loop of 1024 block columns; the live slots of a stripe name distinct blocks. `block_values`: the matrix assembled from the live slots is symmetric: live block (r, c) is the transpose of live block (c, r).
All inputs are finite; a program needn't handle non-finite values.
Results may differ from a plain program's by a relative error of at most 0.002.
The roundings to bfloat16 on the way count: a program that leaves them out, or rounds other values in their place, can miss the bound.
Values may be sent and summed in bfloat16 or wider, within the bound.
No kernel may reach another device: no remote copies, remote signals or barrier semaphores. Data moves between devices by JAX's collectives and lax.ppermute only.
A program may use at most 64 MiB of HBM per device.

v0:
```python
import math
import jax
import jax.numpy as jnp
from jax import lax
from jax.sharding import PartitionSpec as P


def extended_2(cells, sides, width):
    for axis, dim in sides:
        count = lax.axis_size(axis)
        head = lax.slice_in_dim(cells, 0, width, axis=dim)
        tail = lax.slice_in_dim(cells, cells.shape[dim] - width, cells.shape[dim], axis=dim)
        cells = jnp.concatenate(
            [
                lax.ppermute(tail, axis, [(i, (i + 1) % count) for i in range(count)]),
                cells,
                lax.ppermute(head, axis, [((i + 1) % count, i) for i in range(count)]),
            ],
            axis=dim,
        )
    return cells


def propagate(extended, block_values, local_index, placing, precise):
    channels = extended.shape[0]
    block_size = block_values.shape[1]
    blocked = extended.reshape(channels, extended.shape[1] // block_size, block_size)
    gathered = jnp.take(blocked, local_index, axis=1)
    if precise:
        products = jnp.einsum(
            "csb,sab->csa",
            gathered,
            block_values.astype(jnp.float32),
            precision=lax.Precision.HIGHEST,
        )
    else:
        products = jnp.einsum(
            "csb,sab->csa", gathered, block_values, preferred_element_type=jnp.float32
        )
    placed = jnp.einsum("csa,sr->cra", products, placing, precision=lax.Precision.HIGHEST)
    return placed.reshape(channels, placing.shape[1] * block_size)


def activation(entry_value):
    return jax.nn.gelu(entry_value, approximate=True)


def on_device(
    features, block_values, block_rows, block_cols, block_count, labels, weight_in, weight_out
):
    device_count = lax.axis_size("blk")
    stripe_index = lax.axis_index("blk")
    block_size = block_values.shape[1]
    slot_count = block_rows.shape[0]
    stripe_rows = features.shape[1]
    stripe_blocks = stripe_rows // block_size
    reach_blocks = (slot_count // stripe_blocks - 1) // 2
    total_blocks = stripe_blocks * device_count
    local_index = jnp.mod(block_cols - (stripe_index * stripe_blocks - reach_blocks), total_blocks)
    live_slots = jnp.arange(slot_count, dtype=jnp.int32) < block_count[0]
    placing = (
        (block_rows[:, None] == jnp.arange(stripe_blocks, dtype=jnp.int32)[None, :])
        & live_slots[:, None]
    ).astype(jnp.float32)
    band_width = reach_blocks * block_size
    node_scale = 1.0 / math.sqrt(device_count * stripe_rows)
    input_ext = extended_2(features, (("blk", 1),), band_width)
    prop_in = propagate(input_ext, block_values, local_index, placing, False).astype(jnp.bfloat16)
    prop_rows_in = lax.all_to_all(prop_in, "feat", split_axis=1, concat_axis=0, tiled=True)
    pre_hidden = jnp.einsum(
        "ih,ir->hr", weight_in, prop_rows_in, preferred_element_type=jnp.float32
    )
    hidden = activation(pre_hidden).astype(jnp.bfloat16)
    hidden_cols = lax.all_to_all(hidden, "feat", split_axis=0, concat_axis=1, tiled=True)
    hidden_ext = extended_2(hidden_cols, (("blk", 1),), band_width)
    prop_hid = propagate(hidden_ext, block_values, local_index, placing, False).astype(jnp.bfloat16)
    prop_rows_hid = lax.all_to_all(prop_hid, "feat", split_axis=1, concat_axis=0, tiled=True)
    logits = jnp.einsum("hc,hr->cr", weight_out, prop_rows_hid, preferred_element_type=jnp.float32)
    class_count = weight_out.shape[1]
    shifted = logits - jnp.max(logits, axis=0, keepdims=True)
    exponent = jnp.exp(shifted)
    probability = exponent / jnp.sum(exponent, axis=0, keepdims=True)
    onehot = (labels[None, :] == jnp.arange(class_count, dtype=jnp.int32)[:, None]).astype(
        jnp.float32
    )
    dlogits = ((probability - onehot) * node_scale).astype(jnp.bfloat16)
    out_share = jnp.einsum("hr,cr->hc", prop_rows_hid, dlogits, preferred_element_type=jnp.float32)
    grad_out = lax.psum(out_share, ("blk", "feat"))
    back_rows = jnp.einsum("hc,cr->hr", weight_out, dlogits, preferred_element_type=jnp.float32)
    back_cols = lax.all_to_all(
        back_rows.astype(jnp.bfloat16), "feat", split_axis=0, concat_axis=1, tiled=True
    ).astype(back_rows.dtype)
    back_ext = extended_2(back_cols.astype(jnp.bfloat16), (("blk", 1),), band_width).astype(
        back_cols.dtype
    )
    back_prop = propagate(back_ext, block_values, local_index, placing, True)
    back_hid = lax.all_to_all(
        back_prop.astype(jnp.bfloat16), "feat", split_axis=1, concat_axis=0, tiled=True
    ).astype(back_prop.dtype)
    unused_output, pullback = jax.vjp(activation, pre_hidden)
    grad_pre = pullback(back_hid)[0].astype(jnp.bfloat16)
    in_share = jnp.einsum("ir,hr->ih", prop_rows_in, grad_pre, preferred_element_type=jnp.float32)
    grad_in = lax.psum(in_share, ("blk", "feat"))
    return (logits, grad_in, grad_out)


def solution(mesh):
    placed = (
        P("feat", "blk"),
        P("blk", None, None),
        P("blk"),
        P("blk"),
        P("blk"),
        P(("blk", "feat")),
        P(),
        P(),
    )
    return jax.shard_map(
        on_device,
        mesh=mesh,
        in_specs=placed,
        out_specs=(P(None, ("blk", "feat")), P(), P()),
        check_vma=False,
    )
```

profile of v0, /device:TPU:2, one launch (start us, length us, event | category | flops | bytes accessed | tf_op | source)
XLA Modules:
  0.0 618.4 jit_solution(3650204196831870399)
XLA Ops:
  7.2 3.5 collective-permute-start
  10.7 6.3 %collective-permute-start.1 = (bf16[64,1024]{1,0:T(8,128)(2,1)}, bf16[64,1024]{1,0:T(8,128)(2,1)S(1)}, u32[]{:S(2)}, u32[]{:S(2)}) collective-permute-start(bf16[64,1024]{1,0:T(8,128)(2,1)} %param.10), channel_id=1, source_target_pairs={{4,0},{8,4},{12,8},{16,12},{20,16},{24,20},{28,24},{32,28},{36,32}... | collective-permute-start | bytes 393224 | tf_op jit(solution)/shard_map/ppermute | solution.py:17
  17.7 0.7 compare_and_fusion
  18.4 1.4 collective-permute-done.1
  19.9 1.0 copy_bitcast_fusion
  20.9 1.0 gather_fusion.1
  21.9 5.4 fusion.19
  27.3 4.0 fusion.43
  31.4 7.0 %all_to_all.80 = bf16[64,4,256]{2,0,1:T(8,128)(2,1)S(1)} all-to-all(bf16[64,4,256]{2,0,1:T(8,128)(2,1)S(1)} %copy.36), channel_id=1, replica_groups=mesh['blk'=128,'feat'=4] {'feat'}, dimensions={1} | all-to-all | bytes 262144 | tf_op jit(solution)/shard_map/all_to_all | solution.py:69
  38.7 7.0 %all_to_all.81 = bf16[4,64,256]{2,1,0:T(8,128)(2,1)S(1)} all-to-all(bf16[4,64,256]{2,1,0:T(8,128)(2,1)S(1)} %bitcast.120), channel_id=1, replica_groups=mesh['blk'=128,'feat'=4] {'feat'}, dimensions={0} | all-to-all | bytes 262144 | tf_op jit(solution)/shard_map/all_to_all | solution.py:74
  45.7 11.1 %collective-permute-start.3 = (bf16[64,1024]{1,0:T(8,128)(2,1)S(1)}, bf16[64,1024]{1,0:T(8,128)(2,1)S(1)}, u32[]{:S(2)}, u32[]{:S(2)}) collective-permute-start(bf16[64,1024]{1,0:T(8,128)(2,1)S(1)} %bitcast.116), channel_id=1, source_target_pairs={{4,0},{8,4},{12,8},{16,12},{20,16},{24,20},{28,24},{32,28},{36,32}... | collective-permute-start | bytes 393224 | tf_op jit(solution)/shard_map/ppermute | solution.py:17
  56.8 2.1 collective-permute-start.2
  59.3 10.4 %collective-permute-done.2 = bf16[64,1024]{1,0:T(8,128)(2,1)S(1)} collective-permute-done((bf16[64,1024]{1,0:T(8,128)(2,1)S(1)}, bf16[64,1024]{1,0:T(8,128)(2,1)S(1)}, u32[]{:S(2)}, u32[]{:S(2)}) %collective-permute-start.2) | collective-permute-done | bytes 131104 | tf_op jit(solution)/shard_map/ppermute | solution.py:15
  69.8 1.0 gather_fusion.2
  70.8 5.4 fusion.22
  76.2 4.0 fusion.40
  80.4 7.0 %all_to_all.82 = bf16[64,4,256]{2,0,1:T(8,128)(2,1)S(1)} all-to-all(bf16[64,4,256]{2,0,1:T(8,128)(2,1)S(1)} %copy.43), channel_id=1, replica_groups=mesh['blk'=128,'feat'=4] {'feat'}, dimensions={1} | all-to-all | bytes 262144 | tf_op jit(solution)/shard_map/all_to_all | solution.py:77
  87.9 7.0 %all_to_all.83 = bf16[4,64,256]{2,1,0:T(8,128)(2,1)S(1)} all-to-all(bf16[4,64,256]{2,1,0:T(8,128)(2,1)S(1)} %bitcast.121), channel_id=1, replica_groups=mesh['blk'=128,'feat'=4] {'feat'}, dimensions={0} | all-to-all | bytes 262144 | tf_op jit(solution)/shard_map/all_to_all | solution.py:90
  94.9 9.6 %collective-permute-start.5 = (bf16[64,1024]{1,0:T(8,128)(2,1)S(1)}, bf16[64,1024]{1,0:T(8,128)(2,1)S(1)}, u32[]{:S(2)}, u32[]{:S(2)}) collective-permute-start(bf16[64,1024]{1,0:T(8,128)(2,1)S(1)} %bitcast.118), channel_id=1, source_target_pairs={{4,0},{8,4},{12,8},{16,12},{20,16},{24,20},{28,24},{32,28},{36,32}... | collective-permute-start | bytes 393224 | tf_op jit(solution)/shard_map/ppermute | solution.py:17
  104.5 2.1 collective-permute-start.4
  107.1 4.3 collective-permute-done.4
  111.5 2.9 gather_fusion
  114.4 11.1 %fusion.25 = f32[64,136,128]{2,0,1:T(8,128)S(1)} fusion(bf16[136,128,128]{2,1,0:T(8,128)(2,1)} %param.11, f32[136,64,128]{2,1,0:T(8,128)} %gather_fusion, pred[136]{0:T(512)(128)(4,1)S(1)} %get-tuple-element.6), kind=kOutput, calls=%fused_computation.24 | convolution fusion | flops 1712390144 | bytes 13369480 | tf_op jit(solution)/shard_map/csb,sab->csa/dot_general | solution.py:30
  125.4 4.0 fusion.37
  129.6 0.7 copy.50
  130.2 3.3 all-to-all-start.4
  133.6 0.9 fusion.74
  134.5 3.7 all-to-all-done.4
  138.3 0.9 fusion.76
  139.3 469.0 %all-reduce.3.cloned.1.call-done = (f32[256,256]{1,0:T(8,128)}, f32[256,128]{1,0:T(8,128)}) async-done(((f32[256,256]{1,0:T(8,128)}, f32[256,128]{1,0:T(8,128)}), (f32[256,256]{1,0:T(8,128)}, f32[256,128]{1,0:T(8,128)})) %all-reduce.3.cloned.1.call-update) | async-done | bytes 393232 | tf_op jit(solution)/shard_map/psum | solution.py:103
  608.3 1.7 copy.84
  610.0 1.6 copy.85
  (41 shorter events, 2.3 us)
Async XLA Ops:
  7.2 31.2 %copy-start = (bf16[256,256]{1,0:T(8,128)(2,1)S(1)}, bf16[256,256]{1,0:T(8,128)(2,1)}, u32[]{:S(2)}) copy-start(bf16[256,256]{1,0:T(8,128)(2,1)} %param.16) | copy-start | bytes 393220
  7.2 11.2 %collective-permute-start = (bf16[64,1024]{1,0:T(8,128)(2,1)}, bf16[64,1024]{1,0:T(8,128)(2,1)S(1)}, u32[]{:S(2)}, u32[]{:S(2)}) collective-permute-start(bf16[64,1024]{1,0:T(8,128)(2,1)} %param.10), channel_id=1, source_target_pairs={{0,4},{4,8},{8,12},{12,16},{16,20},{20,24},{24,28},{28,32},{32,36}... | collective-permute-start | bytes 393224 | tf_op jit(solution)/shard_map/ppermute | solution.py:15
  10.7 9.1 %collective-permute-start.1 = (bf16[64,1024]{1,0:T(8,128)(2,1)}, bf16[64,1024]{1,0:T(8,128)(2,1)S(1)}, u32[]{:S(2)}, u32[]{:S(2)}) collective-permute-start(bf16[64,1024]{1,0:T(8,128)(2,1)} %param.10), channel_id=1, source_target_pairs={{4,0},{8,4},{12,8},{16,12},{20,16},{24,20},{28,24},{32,28},{36,32}... | collective-permute-start | bytes 393224 | tf_op jit(solution)/shard_map/ppermute | solution.py:17
  21.9 5.4 copy-start.3
  45.7 13.6 %collective-permute-start.3 = (bf16[64,1024]{1,0:T(8,128)(2,1)S(1)}, bf16[64,1024]{1,0:T(8,128)(2,1)S(1)}, u32[]{:S(2)}, u32[]{:S(2)}) collective-permute-start(bf16[64,1024]{1,0:T(8,128)(2,1)S(1)} %bitcast.116), channel_id=1, source_target_pairs={{4,0},{8,4},{12,8},{16,12},{20,16},{24,20},{28,24},{32,28},{36,32}... | collective-permute-start | bytes 393224 | tf_op jit(solution)/shard_map/ppermute | solution.py:17
  56.8 12.9 %collective-permute-start.2 = (bf16[64,1024]{1,0:T(8,128)(2,1)S(1)}, bf16[64,1024]{1,0:T(8,128)(2,1)S(1)}, u32[]{:S(2)}, u32[]{:S(2)}) collective-permute-start(bf16[64,1024]{1,0:T(8,128)(2,1)S(1)} %bitcast.117), channel_id=1, source_target_pairs={{0,4},{4,8},{8,12},{12,16},{16,20},{20,24},{24,28},{28,32},{32,36}... | collective-permute-start | bytes 393224 | tf_op jit(solution)/shard_map/ppermute | solution.py:15
  76.2 11.2 %copy-start.2 = (bf16[256,128]{1,0:T(8,128)(2,1)S(1)}, bf16[256,128]{1,0:T(8,128)(2,1)}, u32[]{:S(2)}) copy-start(bf16[256,128]{1,0:T(8,128)(2,1)} %param.17) | copy-start | bytes 196612
  76.2 11.5 %copy-start.4 = (s32[256]{0:T(256)S(1)}, s32[256]{0:T(256)}, u32[]{:S(2)}) copy-start(s32[256]{0:T(256)} %param.15) | copy-start | bytes 3076
  87.6 46.0 %copy-start.1 = (f32[256,128]{0,1:T(8,128)}, f32[256,128]{0,1:T(8,128)S(1)}, u32[]{:S(2)}) copy-start(f32[256,128]{0,1:T(8,128)S(1)} %get-tuple-element.11) | copy-start | bytes 393220
  94.9 12.2 %collective-permute-start.5 = (bf16[64,1024]{1,0:T(8,128)(2,1)S(1)}, bf16[64,1024]{1,0:T(8,128)(2,1)S(1)}, u32[]{:S(2)}, u32[]{:S(2)}) collective-permute-start(bf16[64,1024]{1,0:T(8,128)(2,1)S(1)} %bitcast.118), channel_id=1, source_target_pairs={{4,0},{8,4},{12,8},{16,12},{20,16},{24,20},{28,24},{32,28},{36,32}... | collective-permute-start | bytes 393224 | tf_op jit(solution)/shard_map/ppermute | solution.py:17
  104.5 6.9 %collective-permute-start.4 = (bf16[64,1024]{1,0:T(8,128)(2,1)S(1)}, bf16[64,1024]{1,0:T(8,128)(2,1)S(1)}, u32[]{:S(2)}, u32[]{:S(2)}) collective-permute-start(bf16[64,1024]{1,0:T(8,128)(2,1)S(1)} %bitcast.119), channel_id=1, source_target_pairs={{0,4},{4,8},{8,12},{12,16},{16,20},{20,24},{24,28},{28,32},{32,36}... | collective-permute-start | bytes 393224 | tf_op jit(solution)/shard_map/ppermute | solution.py:15
  130.2 7.9 %all-to-all-start.4 = ((bf16[64,4,256]{2,0,1:T(8,128)(2,1)}), bf16[64,4,256]{2,0,1:T(8,128)(2,1)S(1)}, u32[]{:S(2)}, u32[]{:S(2)}) async-start(bf16[64,4,256]{2,0,1:T(8,128)(2,1)} %copy.50), calls=%async_computation.4 | async-start | bytes 262144 | tf_op jit(solution)/shard_map/all_to_all | solution.py:97
  133.6 474.8 %all-reduce.3.cloned.1.call-start = ((), (), s32[]{:S(2)}) async-start(), calls=%async_computation.5 | async-start | bytes 786432 | tf_op jit(solution)/shard_map/psum | solution.py:103
Sparse Core Ops, SparseCore 0:
  140.4 467.8 all-reduce.2
where the time goes:
time: 619 us; the launch traced here: 618 us
  waiting for transfers between devices  489 us (79%)
  starting transfers between devices  38.2 us (6%)
  matrix products  36.4 us (6%)
  blocking collectives  28 us (5%)
  between operations  15 us (2%)
  local copies, waits for them, and re-layouts  9.57 us (2%)
    psum x1, waiting for transfers between devices, on_device(): grad_in = lax.psum(in_share, ('blk', 'feat'))  469 us
    ppermute x3, starting transfers between devices, extended_2(): lax.ppermute(head, axis, [((i + 1) % count, i) for i in range(count)])  27.1 us
    ppermute x3, waiting for transfers between devices, extended_2(): lax.ppermute(tail, axis, [(i, (i + 1) % count) for i in range(count)])  14.8 us
  transfers between devices with their start and end apart: 8, of which 7 were waited for; matrix products, arithmetic and copies ran while one was open for 0% of the time, Pallas kernels for 0%

commit v1 on v0

--- a/solution.py
+++ b/solution.py
@@ -100,7 +100,8 @@
     unused_output, pullback = jax.vjp(activation, pre_hidden)
     grad_pre = pullback(back_hid)[0].astype(jnp.bfloat16)
     in_share = jnp.einsum("ir,hr->ih", prop_rows_in, grad_pre, preferred_element_type=jnp.float32)
-    grad_in = lax.psum(in_share, ("blk", "feat"))
+    partial = lax.psum(in_share, "feat")
+    grad_in = lax.psum(partial, "blk")
     return (logits, grad_in, grad_out)
 
 

time: 619 us -> 1880 us (3.04)
  the two profiles are of different devices: /device:TPU:2 before, /device:TPU:24 now
where the time goes in v1:
time: 1880 us
  waiting for transfers between devices  1750 us (93%)
  matrix products  36.4 us (2%)
  starting transfers between devices  34.5 us (2%)
  blocking collectives  33 us (2%)
    psum x1, waiting for transfers between devices, on_device(): grad_in = lax.psum(partial, 'blk')  1220 us
    psum x1, waiting for transfers between devices, on_device(): grad_out = lax.psum(out_share, ('blk', 'feat'))  462 us
    psum x1, waiting for transfers between devices, on_device(): partial = lax.psum(in_share, 'feat')  39.5 us
  transfers between devices with their start and end apart: 9, of which 9 were waited for; matrix products, arithmetic and copies ran while one was open for 0% of the time, Pallas kernels for 0%

profile of v1, /device:TPU:24, one launch (start us, length us, event | category | flops | bytes accessed | tf_op | source)
XLA Modules:
  0.0 1876.1 jit_solution(6624902987727202647)
XLA Ops:
  7.2 3.4 collective-permute-start
  10.6 12.8 collective-permute-start.1
  25.2 1.3 collective-permute-done.1
  26.5 1.0 copy_bitcast_fusion
  27.5 1.0 gather_fusion.1
  28.5 5.4 fusion.19
  33.9 4.0 fusion.43
  38.0 6.1 all_to_all.80
  44.4 7.0 all_to_all.81
  51.4 10.0 collective-permute-start.3
  61.4 2.1 collective-permute-start.2
  64.2 9.8 collective-permute-done.2
  74.1 1.0 gather_fusion.2
  75.1 5.4 fusion.22
  80.5 4.0 fusion.40
  84.7 6.3 all_to_all.82
  91.5 7.0 all_to_all.83
  98.5 2.1 collective-permute-start.5
  100.6 4.0 collective-permute-start.4
  104.8 0.9 collective-permute-done.5
  105.7 7.6 collective-permute-done.4
  113.4 2.9 gather_fusion
  116.3 11.1 fusion.25
  127.4 4.0 fusion.37
  131.5 6.7 all_to_all.84
  138.4 0.9 fusion.76
  139.4 0.9 fusion.74
  140.3 39.5 %all-reduce.4.cloned.1.call-done = f32[256,256]{1,0:T(8,128)} async-done(((f32[256,256]{1,0:T(8,128)}), f32[256,256]{1,0:T(8,128)}) %all-reduce.4.cloned.1.call-update) | async-done | bytes 262160 | tf_op jit(solution)/shard_map/psum | solution.py:103
  179.8 461.9 %all-reduce.8.cloned.1.call-done = f32[256,128]{1,0:T(8,128)} async-done(((f32[256,128]{1,0:T(8,128)}), f32[256,128]{1,0:T(8,128)}) %all-reduce.8.cloned.1.call-update) | async-done | bytes 131088 | tf_op jit(solution)/shard_map/psum | solution.py:88
  641.8 1224.5 %all-reduce.6.cloned.1.call-done = f32[256,256]{1,0:T(8,128)} async-done(((f32[256,256]{1,0:T(8,128)}), f32[256,256]{1,0:T(8,128)}) %all-reduce.6.cloned.1.call-update) | async-done | bytes 262160 | tf_op jit(solution)/shard_map/psum | solution.py:104
  1866.3 1.7 copy.85
  1868.0 1.6 copy.86
  (46 shorter events, 3.7 us)
Async XLA Ops:
  7.2 36.9 %copy-start = (bf16[256,256]{1,0:T(8,128)(2,1)S(1)}, bf16[256,256]{1,0:T(8,128)(2,1)}, u32[]{:S(2)}) copy-start(bf16[256,256]{1,0:T(8,128)(2,1)} %param.16) | copy-start | bytes 393220
  7.2 172.6 %all-reduce.4.cloned.1.call-start = ((), (), s32[]{:S(2)}) async-start(), calls=%async_computation.5 | async-start | bytes 524288 | tf_op jit(solution)/shard_map/psum | solution.py:103
  7.2 18.0 collective-permute-start
  10.6 15.8 collective-permute-start.1
  28.5 5.4 copy-start.3
  51.4 12.8 collective-permute-start.3
  61.4 12.6 collective-permute-start.2
  80.5 10.5 copy-start.2
  80.5 10.8 copy-start.4
  91.2 48.2 %copy-start.1 = (f32[256,128]{0,1:T(8,128)}, f32[256,128]{0,1:T(8,128)S(1)}, u32[]{:S(2)}) copy-start(f32[256,128]{0,1:T(8,128)S(1)} %get-tuple-element.9) | copy-start | bytes 393220
  98.5 7.2 collective-permute-start.5
  100.6 12.7 collective-permute-start.4
  139.3 502.4 %all-reduce.8.cloned.1.call-start = ((), (), s32[]{:S(2)}) async-start(), calls=%async_computation.7 | async-start | bytes 262144 | tf_op jit(solution)/shard_map/psum | solution.py:88
  140.3 1726.0 %all-reduce.6.cloned.1.call-start = ((), (), s32[]{:S(2)}) async-start(), calls=%async_computation.6 | async-start | bytes 524288 | tf_op jit(solution)/shard_map/psum | solution.py:104
Sparse Core Ops, SparseCore 0:
  139.5 40.2 all-reduce.3
  185.8 455.8 all-reduce.7
  644.7 1221.5 all-reduce.5
